TPU v7x, 256 devices: a whole 4x4x8 slice. The times are simulated.
256 devices in a mesh: dom: 32 (over y_lo, z, core), repl: 8 (over y_hi, x).
Axes of the slice: x: 4, y: 4 (y_hi: 2, y_lo: 2; y = y_hi * 2 + y_lo), z: 8, core: 2. Of those that a mesh axis runs over, the one named last changes fastest.
Arguments:
- features: float32 [131072, 256], P(('dom', 'repl')), may hold values from -6 to 6
- weight: bfloat16 [256, 256], replicated, may hold values from -0.375 to 0.375
- bias_vector: float32 [256], replicated, may hold values from -0.5 to 0.5
- cotangent: bfloat16 [131072, 256], P(('dom', 'repl')), may hold values from -6 to 6
- near_tiles: bfloat16 [4096, 128, 128], P(('dom', 'repl')), may hold values from -0.1875 to 0.1875
- near_offsets: int32 [256, 33], P(('dom', 'repl')), may hold values from 0 to 16, as said below
- near_cols: int32 [256, 16], P(('dom', 'repl')), may hold values from 0 to 3, as said below
- far_tiles: bfloat16 [256, 32, 1, 128, 128], P(('dom', 'repl')), may hold values from -0.1875 to 0.1875
- far_rows: int32 [256, 32, 1], P(('dom', 'repl')), may hold values from -1 to 31, as said below
- far_cols: int32 [256, 32, 1], P(('dom', 'repl')), may hold values from 0 to 3
Outputs:
- hidden: bfloat16 [131072, 256], P(('dom', 'repl'))
- grad_features: float32 [131072, 256], P(('dom', 'repl'))
- weight_grad: float32 [256, 256], replicated
Inputs may be any that keep to these rules, and one draw needn't show every extreme that they name: `near_offsets`: each row is non-decreasing, begins with 0 and ends with 16. `near_cols`: within one tile row of one device the near tiles' columns differ and rise. `far_rows`: -1 marks an empty slot. A device's slots for the groups whose index of dom lies at most 2 steps from its own around the cycle are never empty.
All inputs are finite; a program needn't handle non-finite values.
Results may differ from a plain program's by a relative error of at most 0.0075.
Values may be sent and summed in bfloat16 or wider, within the bound.
No kernel may reach another device: no remote copies, remote signals or barrier semaphores. Data moves between devices by JAX's collectives and lax.ppermute only.
A program may use at most 128 MiB of HBM per device.

v0:
```python
import math
import jax
import jax.numpy as jnp
from jax import lax
from jax.sharding import PartitionSpec as P


def membership_flags(index, extent, dtype):
    return (index[..., None] == jnp.arange(extent, dtype=jnp.int32)).astype(dtype)


def slot_rows(offsets, slot_count):
    slots = jnp.arange(slot_count, dtype=jnp.int32)
    return jnp.sum((offsets[1:, None] <= slots[None, :]).astype(jnp.int32), axis=0)


def precise_total_sum(form, hot, values):
    return jnp.einsum(form, hot, values, precision=lax.Precision.HIGHEST)


def select(form, hot, values):
    return jnp.einsum(form, hot, values, preferred_element_type=jnp.float32).astype(jnp.bfloat16)


def tile_product(form, tiles, values):
    return jnp.einsum(form, tiles, values, preferred_element_type=jnp.float32)


def activation_grad(pre_values, upstream):
    sigma = jax.nn.sigmoid(pre_values)
    return (upstream.astype(jnp.float32) * sigma * (1.0 + pre_values * (1.0 - sigma))).astype(
        jnp.bfloat16
    )


def on_device(
    features,
    weight,
    bias_vector,
    cotangent,
    near_tiles,
    near_offsets,
    near_cols,
    far_tiles,
    far_rows,
    far_cols,
):
    rows_dev, feat_width = features.shape
    tile_size = near_tiles.shape[1]
    blocks_per_processor = rows_dev // tile_size
    dom_count = lax.axis_size("dom")
    repl_count = lax.axis_size("repl")
    blocks_dom = blocks_per_processor * repl_count
    near_count = near_tiles.shape[0]
    far_block = far_tiles[0]
    far_row_ids = far_rows[0]
    far_col_ids = far_cols[0]
    near_row_ids = slot_rows(near_offsets[0], near_count)
    nearby_column_index = near_cols[0]
    reduced = features.astype(jnp.bfloat16)
    local_block_list = reduced.reshape(blocks_per_processor, tile_size, feat_width)
    nearby_input_rows = select(
        "el,lxh->exh",
        membership_flags(nearby_column_index, blocks_per_processor, jnp.bfloat16),
        local_block_list,
    )
    near_prod = tile_product("qab,qbf->qaf", near_tiles, nearby_input_rows)
    partial_sum = precise_total_sum(
        "qr,qaf->raf", membership_flags(near_row_ids, blocks_dom, jnp.float32), near_prod
    )
    shard_rows = lax.all_gather(reduced, "dom", axis=0, tiled=True)
    range_count = shard_rows.shape[0] // rows_dev
    tiles = far_block
    row_ids = far_row_ids
    col_ids = far_col_ids
    source = shard_rows.reshape(range_count, blocks_per_processor, tile_size, feat_width)
    inputs = select(
        "kqc,kcbf->kqbf", membership_flags(col_ids, blocks_per_processor, jnp.bfloat16), source
    )
    far_prod = tile_product("kqab,kqbf->kqaf", tiles, inputs)
    partial_sum = partial_sum + precise_total_sum(
        "kqr,kqaf->raf", membership_flags(row_ids, blocks_dom, jnp.float32), far_prod
    )
    group_partial = partial_sum.reshape(blocks_dom * tile_size, feat_width)
    summed = lax.psum_scatter(group_partial, "repl", scatter_dimension=0, tiled=True).astype(
        jnp.bfloat16
    )
    pre_act = jnp.dot(summed, weight, preferred_element_type=jnp.float32) + bias_vector
    hidden = jax.nn.silu(pre_act).astype(jnp.bfloat16)
    grad_pre = activation_grad(pre_act, cotangent)
    weight_term = lax.dot_general(
        summed, grad_pre, (((0,), (0,)), ((), ())), preferred_element_type=jnp.float32
    )
    grad_rows = lax.dot_general(
        grad_pre, weight, (((1,), (1,)), ((), ())), preferred_element_type=jnp.float32
    ).astype(jnp.bfloat16)
    group_grad = lax.all_gather(grad_rows, "repl", axis=0, tiled=True)
    node_total = rows_dev * dom_count * repl_count
    weight_grad = lax.psum(weight_term, ("dom", "repl")) * (1.0 / math.sqrt(node_total))
    cluster_block_list = group_grad.reshape(blocks_dom, tile_size, feat_width)
    near_grads = select(
        "om,mgh->ogh", membership_flags(near_row_ids, blocks_dom, jnp.bfloat16), cluster_block_list
    )
    nearby_backward_pass = tile_product("ltp,ltk->lpk", near_tiles, near_grads)
    local_contribution = precise_total_sum(
        "ml,mrx->lrx",
        membership_flags(nearby_column_index, blocks_per_processor, jnp.float32),
        nearby_backward_pass,
    )
    row_count = rows_dev * lax.axis_size("dom")
    tiles = far_block
    row_ids = far_row_ids
    col_ids = far_col_ids
    far_grads = select(
        "kqr,rbf->kqbf", membership_flags(row_ids, blocks_dom, jnp.bfloat16), cluster_block_list
    )
    terms = tile_product("kqab,kqaf->kqbf", tiles, far_grads)
    placed = precise_total_sum(
        "kqc,kqbf->kcbf", membership_flags(col_ids, blocks_per_processor, jnp.float32), terms
    )
    far_grad = lax.psum_scatter(
        placed.reshape(row_count, feat_width).astype(jnp.bfloat16),
        "dom",
        scatter_dimension=0,
        tiled=True,
    ).astype(jnp.float32)
    grad_features = far_grad + local_contribution.reshape(rows_dev, feat_width)
    return (hidden, grad_features, weight_grad)


def solution(mesh):
    placed = (
        P(("dom", "repl"), None),
        P(),
        P(),
        P(("dom", "repl"), None),
        P(("dom", "repl"), None, None),
        P(("dom", "repl"), None),
        P(("dom", "repl"), None),
        P(("dom", "repl"), None, None, None, None),
        P(("dom", "repl"), None, None),
        P(("dom", "repl"), None, None),
    )
    return jax.shard_map(
        on_device,
        mesh=mesh,
        in_specs=placed,
        out_specs=(P(("dom", "repl"), None), P(("dom", "repl"), None), P()),
        check_vma=False,
    )
```

profile of v0, /device:TPU:2, one launch (start us, length us, event | category | flops | bytes accessed | tf_op | source)
XLA Modules:
  0.0 674.9 jit_solution(15560080894403100846)
XLA Ops:
  7.2 0.0 copy-start
  7.2 0.0 copy-start.2
  7.2 0.0 all-gather.3.cloned.1.call-start
  7.2 1.9 convert_element_type.53
  9.1 0.0 all-gather.3.cloned.1.call-update
  9.2 0.0 reduce-scatter.3.cloned.1.call-start
  9.2 1.5 convolution_convert_fusion.1
  10.7 0.0 copy-done.2
  10.7 1.9 convolution_bitcast_fusion.3
  12.6 2.3 copy.19
  14.9 0.0 copy-done.11
  14.9 0.1 slice_bitcast_fusion
  15.0 0.1 convert_reduce_fusion
  15.1 0.1 fusion.18
  15.2 3.6 fusion.28
  18.7 66.3 %all-gather.3.cloned.1.call-done = bf16[16384,256]{1,0:T(8,128)(2,1)} async-done(((bf16[512,256]{1,0:T(8,128)(2,1)}), bf16[16384,256]{1,0:T(8,128)(2,1)}) %all-gather.3.cloned.1.call-update) | async-done | bytes 8388624 | tf_op jit(solution)/shard_map/all_gather | solution.py:71
  85.0 11.8 %fusion = bf16[32,1,128,256]{3,1,2,0:T(2,128)(2,1)} fusion(bf16[32,4,128,256]{3,2,1,0:T(8,128)(2,1)} %bitcast.65, pred[32,4,1,1]{1,0,2,3:T(32,128)(4,1)S(1)} %get-tuple-element.6), kind=kOutput, calls=%fused_computation.1 | convolution fusion | flops 8388608 | bytes 10485888 | tf_op jit(solution)/shard_map/kqc,kcbf->kqbf/dot_general | solution.py:22
  96.8 8.6 %copy.31 = bf16[32,1,128,256]{2,3,0,1:T(8,128)(2,1)S(1)} copy(bf16[32,1,128,256]{3,1,2,0:T(2,128)(2,1)} %fusion) | data formatting | bytes 4194304 | tf_op jit(solution)/shard_map/kqc,kcbf->kqbf/dot_general | solution.py:22
  105.4 2.7 convolution_bitcast_fusion.1
  108.1 5.5 copy.20
  113.6 5.7 convolution_add_fusion
  119.3 4.4 copy.21
  123.7 0.0 reduce-scatter.3.cloned.1.call-update
  123.7 0.0 all-gather.5.cloned.1.call-start
  123.8 89.6 %reduce-scatter.3.cloned.1.call-done = f32[512,256]{1,0:T(8,128)} async-done(((f32[4096,256]{1,0:T(8,128)}), f32[512,256]{1,0:T(8,128)}) %reduce-scatter.3.cloned.1.call-update) | async-done | bytes 524304 | tf_op jit(solution)/shard_map/reduce_scatter | solution.py:85
  213.4 2.2 multiply_convert_fusion.1
  215.7 1.0 convolution_convert_fusion.2
  216.6 0.0 all-gather.5.cloned.1.call-update
  216.7 0.2 all-reduce.2.cloned.1.call-start
  216.9 1.0 fusion.14
  217.9 0.0 all-reduce.2.cloned.1.call-update
  217.9 0.0 reduce-scatter.5.cloned.1.call-start
  218.0 57.9 %all-gather.5.cloned.1.call-done = bf16[4096,256]{1,0:T(8,128)(2,1)} async-done(((bf16[512,256]{1,0:T(8,128)(2,1)}), bf16[4096,256]{1,0:T(8,128)(2,1)}) %all-gather.5.cloned.1.call-update) | async-done | bytes 2097168 | tf_op jit(solution)/shard_map/all_gather | solution.py:97
  275.8 2.9 convolution_convert_fusion
  278.8 3.7 convolution_bitcast_fusion
  282.5 5.6 copy.24
  288.1 8.7 %multiply_convert_fusion = bf16[32,4,128,256]{3,2,1,0:T(8,128)(2,1)} fusion(f32[32,128,256]{2,1,0:T(8,128)} %copy.24, f32[32,4]{1,0:T(8,128)S(1)} %get-tuple-element.5), kind=kLoop, calls=%fused_computation | loop fusion | flops 8388608 | bytes 12583424 | tf_op jit(solution)/shard_map/convert_element_type | solution.py:122
  296.8 0.0 reduce-scatter.5.cloned.1.call-update
  296.8 238.4 %all-reduce.2.cloned.1.call-done = f32[256,256]{1,0:T(8,128)} async-done(((f32[256,256]{1,0:T(8,128)}), f32[256,256]{1,0:T(8,128)}) %all-reduce.2.cloned.1.call-update) | async-done | bytes 262160 | tf_op jit(solution)/shard_map/psum | solution.py:99
  535.2 1.7 broadcast_multiply_fusion
  537.0 1.2 fusion.6
  538.2 0.5 convolution_bitcast_fusion.2
  538.7 0.0 copy-start.7
  538.7 2.0 copy.27
  540.8 2.4 fusion.33
  543.2 0.1 copy.28
  543.3 123.3 %reduce-scatter.5.cloned.1.call-done = bf16[512,256]{1,0:T(8,128)(2,1)} async-done(((bf16[16384,256]{1,0:T(8,128)(2,1)}), bf16[512,256]{1,0:T(8,128)(2,1)}) %reduce-scatter.5.cloned.1.call-update) | async-done | bytes 262160 | tf_op jit(solution)/shard_map/reduce_scatter | solution.py:121
  666.6 1.8 bitcast_add_fusion
  (19 shorter events, 0.0 us)
Async XLA Ops:
  7.2 98.3 %copy-start = (bf16[1,32,1,128,128]{4,3,2,1,0:T(8,128)(2,1)S(1)}, bf16[1,32,1,128,128]{4,3,2,1,0:T(8,128)(2,1)}, u32[]{:S(2)}) copy-start(bf16[1,32,1,128,128]{4,3,2,1,0:T(8,128)(2,1)} %param.17) | copy-start | bytes 3145732
  7.2 3.5 copy-start.2
  7.2 77.8 %all-gather.3.cloned.1.call-start = ((), (), s32[]{:S(2)}) async-start(), calls=%async_computation.2 | async-start | bytes 8650752 | tf_op jit(solution)/shard_map/all_gather | solution.py:71
  9.2 204.3 %reduce-scatter.3.cloned.1.call-start = ((), (), s32[]{:S(2)}) async-start(), calls=%async_computation.3 | async-start | bytes 4718592 | tf_op jit(solution)/shard_map/reduce_scatter | solution.py:85
  12.6 2.3 copy-start.11
  12.6 2.5 copy-start.8
  108.1 5.5 copy-start.6
  123.7 89.7 %copy-start.5 = (bf16[256,256]{1,0:T(8,128)(2,1)S(1)}, bf16[256,256]{1,0:T(8,128)(2,1)}, u32[]{:S(2)}) copy-start(bf16[256,256]{1,0:T(8,128)(2,1)} %param.11) | copy-start | bytes 393220
  123.7 89.7 %copy-start.9 = (bf16[512,256]{1,0:T(8,128)(2,1)S(1)}, bf16[512,256]{1,0:T(8,128)(2,1)}, u32[]{:S(2)}) copy-start(bf16[512,256]{1,0:T(8,128)(2,1)} %param.13) | copy-start | bytes 786436
  123.7 89.7 %copy-start.10 = (f32[256]{0:T(256)S(1)}, f32[256]{0:T(256)}, u32[]{:S(2)}) copy-start(f32[256]{0:T(256)} %param.12) | copy-start | bytes 3076
  123.7 152.1 %all-gather.5.cloned.1.call-start = ((), (), s32[]{:S(2)}) async-start(), calls=%async_computation.4 | async-start | bytes 2359296 | tf_op jit(solution)/shard_map/all_gather | solution.py:97
  213.4 3.5 copy-start.4
  216.7 318.5 %all-reduce.2.cloned.1.call-start = ((), (), s32[]{:S(2)}) async-start(), calls=%async_computation.6 | async-start | bytes 524288 | tf_op jit(solution)/shard_map/psum | solution.py:99
  217.9 448.7 %reduce-scatter.5.cloned.1.call-start = ((), (), s32[]{:S(2)}) async-start(), calls=%async_computation.5 | async-start | bytes 8650752 | tf_op jit(solution)/shard_map/reduce_scatter | solution.py:121
  296.8 240.1 %copy-start.1 = (bf16[4096,256]{1,0:T(8,128)(2,1)S(1)}, bf16[4096,256]{1,0:T(8,128)(2,1)}, u32[]{:S(2)}) copy-start(bf16[4096,256]{1,0:T(8,128)(2,1)} %all-gather.5.cloned.1.call-done) | copy-start | bytes 6291460
  535.2 3.0 copy-start.3
  538.7 2.0 copy-start.7
Sparse Core Ops, SparseCore 0:
  10.4 74.5 all-gather.2
  123.9 89.5 reduce-scatter.2
  216.8 59.0 all-gather.4
  281.7 253.4 all-reduce.1
  537.6 128.9 reduce-scatter.4
where the time goes:
time: 676 us; the launch traced here: 675 us
  waiting for transfers between devices  576 us (85%)
  matrix products  42.2 us (6%)
  local copies, waits for them, and re-layouts  28.6 us (4%)
  other arithmetic  14.4 us (2%)
  between operations  13.9 us (2%)
    psum x1, waiting for transfers between devices, on_device(): lax.psum(weight_term, ('dom', 'repl')) * (1.0 / math.sqrt(node_total))  238 us
    reduce_scatter x1, waiting for transfers between devices, on_device(): lax.psum_scatter(placed.reshape(row_count, feat_width).astype(jnp.bfloat1...  123 us
    reduce_scatter x1, waiting for transfers between devices, on_device(): lax.psum_scatter(group_partial, 'repl', scatter_dimension=0, tiled=True)  89.6 us
    all_gather x1, waiting for transfers between devices, on_device(): shard_rows = lax.all_gather(reduced, 'dom', axis=0, tiled=True)  66.3 us
    all_gather x1, waiting for transfers between devices, on_device(): group_grad = lax.all_gather(grad_rows, 'repl', axis=0, tiled=True)  57.9 us
    dot_general x4, matrix products, select(): jnp.einsum(form, hot, values, preferred_element_type=jnp.float32)  17.5 us
    dot_general x4, local copies, waits for them, and re-layouts, tile_product(): return jnp.einsum(form, tiles, values, preferred_element_type=jnp.float32)  15.4 us
  transfers between devices with their start and end apart: 5, of which 5 were waited for; matrix products, arithmetic and copies ran while one was open for 6% of the time, Pallas kernels for 0%

commit v1 on v0

--- a/solution.py
+++ b/solution.py
@@ -68,7 +68,15 @@
     partial_sum = precise_total_sum(
         "qr,qaf->raf", membership_flags(near_row_ids, blocks_dom, jnp.float32), near_prod
     )
-    shard_rows = lax.all_gather(reduced, "dom", axis=0, tiled=True)
+    shard_rows = jnp.concatenate(
+        lax.all_to_all(
+            jnp.stack([reduced] * lax.axis_size("dom")),
+            concat_axis=0,
+            axis_name="dom",
+            split_axis=0,
+        ),
+        axis=0,
+    )
     range_count = shard_rows.shape[0] // rows_dev
     tiles = far_block
     row_ids = far_row_ids

time: 676 us -> 801 us (1.18)
  waiting for transfers between devices: 576 us -> 689 us
  starting transfers between devices: 0.39 us -> 10.5 us
    all_to_all x0 -> x1, waiting for transfers between devices: none -> 178 us  [on_device(): lax.all_to_all(jnp.stack([reduced] * lax.axis_size('dom')), concat_axis=0...]
    all_gather x1 -> x0, waiting for transfers between devices: 66.3 us -> none  [on_device(): shard_rows = lax.all_gather(reduced, 'dom', axis=0, tiled=True)]
    all_to_all x0 -> x1, starting transfers between devices: none -> 10.1 us  [on_device(): lax.all_to_all(jnp.stack([reduced] * lax.axis_size('dom')), concat_axis=0...]
  transfers between devices with their start and end apart: 5 -> 5, of which waited for: 5 -> 5; matrix products, arithmetic and copies ran while one was open for 6% -> 5% of each run, Pallas kernels for 0% -> 0%
where the time goes in v1:
time: 801 us
  waiting for transfers between devices  689 us (86%)
  matrix products  41.2 us (5%)
  local copies, waits for them, and re-layouts  32.8 us (4%)
  between operations  13.9 us (2%)
  other arithmetic  13.6 us (2%)
  starting transfers between devices  10.5 us (1%)
    psum x1, waiting for transfers between devices, on_device(): lax.psum(weight_term, ('dom', 'repl')) * (1.0 / math.sqrt(node_total))  239 us
    all_to_all x1, waiting for transfers between devices, on_device(): lax.all_to_all(jnp.stack([reduced] * lax.axis_size('dom')), concat_axis=0...  178 us
    reduce_scatter x1, waiting for transfers between devices, on_device(): lax.psum_scatter(placed.reshape(row_count, feat_width).astype(jnp.bfloat1...  123 us
    reduce_scatter x1, waiting for transfers between devices, on_device(): lax.psum_scatter(group_partial, 'repl', scatter_dimension=0, tiled=True)  91.2 us
    all_gather x1, waiting for transfers between devices, on_device(): group_grad = lax.all_gather(grad_rows, 'repl', axis=0, tiled=True)  57.9 us
    dot_general x4, matrix products, select(): jnp.einsum(form, hot, values, preferred_element_type=jnp.float32)  16.5 us
  transfers between devices with their start and end apart: 5, of which 5 were waited for; matrix products, arithmetic and copies ran while one was open for 5% of the time, Pallas kernels for 0%

profile of v1, /device:TPU:2, one launch (start us, length us, event | category | flops | bytes accessed | tf_op | source)
XLA Modules:
  0.0 800.5 jit_solution(6775724517601051763)
XLA Ops:
  7.2 0.0 copy-start
  7.2 1.2 convert_element_type.53
  8.3 4.2 stack.2
  12.5 10.1 %all-to-all-start = ((bf16[32,512,256]{2,1,0:T(8,128)(2,1)}), bf16[32,512,256]{2,1,0:T(8,128)(2,1)}, u32[]{:S(2)}, u32[]{:S(2)}) async-start(bf16[32,512,256]{2,1,0:T(8,128)(2,1)} %stack.2), calls=%async_computation | async-start | bytes 16777216 | tf_op jit(solution)/shard_map/all_to_all | solution.py:72
  22.7 0.0 reduce-scatter.3.cloned.1.call-start
  22.7 0.0 copy-done.7
  22.7 0.5 convolution_convert_fusion.1
  23.3 1.9 convolution_bitcast_fusion.3
  25.1 2.3 copy.19
  27.4 0.1 slice_bitcast_fusion
  27.5 0.1 convert_reduce_fusion
  27.6 0.1 fusion.18
  27.7 3.6 fusion.28
  31.3 177.5 %all-to-all-done = bf16[32,512,256]{2,1,0:T(8,128)(2,1)} async-done(((bf16[32,512,256]{2,1,0:T(8,128)(2,1)}), bf16[32,512,256]{2,1,0:T(8,128)(2,1)}, u32[]{:S(2)}, u32[]{:S(2)}) %all-to-all-start) | async-done | bytes 8388640 | tf_op jit(solution)/shard_map/all_to_all | solution.py:72
  208.8 11.8 %fusion = bf16[32,1,128,256]{3,1,2,0:T(2,128)(2,1)} fusion(bf16[32,4,128,256]{3,2,1,0:T(8,128)(2,1)} %bitcast.10, pred[32,4,1,1]{1,0,2,3:T(32,128)(4,1)S(1)} %get-tuple-element.6), kind=kOutput, calls=%fused_computation.1 | convolution fusion | flops 8388608 | bytes 10485888 | tf_op jit(solution)/shard_map/kqc,kcbf->kqbf/dot_general | solution.py:22
  220.6 8.6 %copy.31 = bf16[32,1,128,256]{2,3,0,1:T(8,128)(2,1)S(1)} copy(bf16[32,1,128,256]{3,1,2,0:T(2,128)(2,1)} %fusion) | data formatting | bytes 4194304 | tf_op jit(solution)/shard_map/kqc,kcbf->kqbf/dot_general | solution.py:22
  229.2 2.7 convolution_bitcast_fusion.1
  231.9 5.5 copy.20
  237.4 5.7 convolution_add_fusion
  243.1 4.4 copy.21
  247.5 0.0 reduce-scatter.3.cloned.1.call-update
  247.6 0.0 all-gather.2.cloned.1.call-start
  247.6 91.2 %reduce-scatter.3.cloned.1.call-done = f32[512,256]{1,0:T(8,128)} async-done(((f32[4096,256]{1,0:T(8,128)}), f32[512,256]{1,0:T(8,128)}) %reduce-scatter.3.cloned.1.call-update) | async-done | bytes 524304 | tf_op jit(solution)/shard_map/reduce_scatter | solution.py:93
  338.9 0.0 copy-done.10
  338.9 2.2 multiply_convert_fusion.1
  341.1 1.0 convolution_convert_fusion.2
  342.1 0.0 all-gather.2.cloned.1.call-update
  342.1 0.0 all-reduce.2.cloned.1.call-start
  342.1 1.0 fusion.14
  343.1 0.0 all-reduce.2.cloned.1.call-update
  343.1 0.2 reduce-scatter.5.cloned.1.call-start
  343.4 57.9 %all-gather.2.cloned.1.call-done = bf16[4096,256]{1,0:T(8,128)(2,1)} async-done(((bf16[512,256]{1,0:T(8,128)(2,1)}), bf16[4096,256]{1,0:T(8,128)(2,1)}) %all-gather.2.cloned.1.call-update) | async-done | bytes 2097168 | tf_op jit(solution)/shard_map/all_gather | solution.py:105
  401.3 2.9 convolution_convert_fusion
  404.2 3.7 convolution_bitcast_fusion
  407.9 5.6 copy.24
  413.5 8.7 %multiply_convert_fusion = bf16[32,4,128,256]{3,2,1,0:T(8,128)(2,1)} fusion(f32[32,128,256]{2,1,0:T(8,128)} %copy.24, f32[32,4]{1,0:T(8,128)S(1)} %get-tuple-element.5), kind=kLoop, calls=%fused_computation | loop fusion | flops 8388608 | bytes 12583424 | tf_op jit(solution)/shard_map/convert_element_type | solution.py:130
  422.3 0.0 reduce-scatter.5.cloned.1.call-update
  422.3 238.5 %all-reduce.2.cloned.1.call-done = f32[256,256]{1,0:T(8,128)} async-done(((f32[256,256]{1,0:T(8,128)}), f32[256,256]{1,0:T(8,128)}) %all-reduce.2.cloned.1.call-update) | async-done | bytes 262160 | tf_op jit(solution)/shard_map/psum | solution.py:107
  660.8 1.7 broadcast_multiply_fusion
  662.5 0.0 copy-done.1
  662.5 1.2 fusion.6
  663.8 0.0 copy-done.3
  663.8 0.5 convolution_bitcast_fusion.2
  664.3 2.0 copy.27
  666.3 2.4 fusion.33
  668.7 0.1 copy.28
  668.8 123.3 %reduce-scatter.5.cloned.1.call-done = bf16[512,256]{1,0:T(8,128)(2,1)} async-done(((bf16[16384,256]{1,0:T(8,128)(2,1)}), bf16[512,256]{1,0:T(8,128)(2,1)}) %reduce-scatter.5.cloned.1.call-update) | async-done | bytes 262160 | tf_op jit(solution)/shard_map/reduce_scatter | solution.py:129
  792.2 1.8 bitcast_add_fusion
  (19 shorter events, 0.0 us)
Async XLA Ops:
  7.2 222.0 %copy-start = (bf16[1,32,1,128,128]{4,3,2,1,0:T(8,128)(2,1)S(1)}, bf16[1,32,1,128,128]{4,3,2,1,0:T(8,128)(2,1)}, u32[]{:S(2)}) copy-start(bf16[1,32,1,128,128]{4,3,2,1,0:T(8,128)(2,1)} %param.17) | copy-start | bytes 3145732
  12.5 10.2 %copy-start.7 = (s32[1,16]{1,0:T(1,128)S(1)}, s32[1,16]{1,0:T(1,128)}, u32[]{:S(2)}) copy-start(s32[1,16]{1,0:T(1,128)} %param.16) | copy-start | bytes 196
  12.5 10.7 %copy-start.2 = (bf16[16,128,128]{2,1,0:T(8,128)(2,1)S(1)}, bf16[16,128,128]{2,1,0:T(8,128)(2,1)}, u32[]{:S(2)}) copy-start(bf16[16,128,128]{2,1,0:T(8,128)(2,1)} %param.14) | copy-start | bytes 1572868
  12.5 196.3 %all-to-all-start = ((bf16[32,512,256]{2,1,0:T(8,128)(2,1)}), bf16[32,512,256]{2,1,0:T(8,128)(2,1)}, u32[]{:S(2)}, u32[]{:S(2)}) async-start(bf16[32,512,256]{2,1,0:T(8,128)(2,1)} %stack.2), calls=%async_computation | async-start | bytes 16777216 | tf_op jit(solution)/shard_map/all_to_all | solution.py:72
  22.7 316.2 %reduce-scatter.3.cloned.1.call-start = ((), (), s32[]{:S(2)}) async-start(), calls=%async_computation.3 | async-start | bytes 4718592 | tf_op jit(solution)/shard_map/reduce_scatter | solution.py:93
  25.1 2.3 copy-start.11
  25.1 2.5 copy-start.8
  231.9 5.5 copy-start.6
  247.5 91.3 %copy-start.5 = (bf16[256,256]{1,0:T(8,128)(2,1)S(1)}, bf16[256,256]{1,0:T(8,128)(2,1)}, u32[]{:S(2)}) copy-start(bf16[256,256]{1,0:T(8,128)(2,1)} %param.11) | copy-start | bytes 393220
  247.5 91.3 %copy-start.9 = (bf16[512,256]{1,0:T(8,128)(2,1)S(1)}, bf16[512,256]{1,0:T(8,128)(2,1)}, u32[]{:S(2)}) copy-start(bf16[512,256]{1,0:T(8,128)(2,1)} %param.13) | copy-start | bytes 786436
  247.5 91.3 %copy-start.10 = (f32[256]{0:T(256)S(1)}, f32[256]{0:T(256)}, u32[]{:S(2)}) copy-start(f32[256]{0:T(256)} %param.12) | copy-start | bytes 3076
  247.6 153.7 %all-gather.2.cloned.1.call-start = ((), (), s32[]{:S(2)}) async-start(), calls=%async_computation.4 | async-start | bytes 2359296 | tf_op jit(solution)/shard_map/all_gather | solution.py:105
  338.9 3.3 copy-start.4
  342.1 318.7 %all-reduce.2.cloned.1.call-start = ((), (), s32[]{:S(2)}) async-start(), calls=%async_computation.6 | async-start | bytes 524288 | tf_op jit(solution)/shard_map/psum | solution.py:107
  343.1 449.0 %reduce-scatter.5.cloned.1.call-start = ((), (), s32[]{:S(2)}) async-start(), calls=%async_computation.5 | async-start | bytes 8650752 | tf_op jit(solution)/shard_map/reduce_scatter | solution.py:129
  422.2 240.3 %copy-start.1 = (bf16[4096,256]{1,0:T(8,128)(2,1)S(1)}, bf16[4096,256]{1,0:T(8,128)(2,1)}, u32[]{:S(2)}) copy-start(bf16[4096,256]{1,0:T(8,128)(2,1)} %all-gather.2.cloned.1.call-done) | copy-start | bytes 6291460
  660.8 3.0 copy-start.3
Sparse Core Ops, SparseCore 0:
  247.7 91.1 reduce-scatter.2
  342.2 59.0 all-gather.1
  407.3 253.4 all-reduce.1
  663.2 128.9 reduce-scatter.4
